TPU v7x, 512 devices: a whole 4x8x8 slice. The times are simulated.
512 devices in a mesh: rec: 128 (over y, z, core), grp: 4 (over x).
Axes of the slice: x: 4, y: 8, z: 8, core: 2. Of those that a mesh axis runs over, the one named last changes fastest.
Arguments:
- conv_in: bfloat16 [4, 131072, 512], P('grp', 'rec'), may hold values from -6 to 6
- conv5_weight: bfloat16 [1536, 512], P(None, 'grp'), may hold values from -0.15625 to 0.15625
- conv6_weight: bfloat16 [1024, 512], P(None, 'grp'), may hold values from -0.1875 to 0.1875
- conv7_weight: bfloat16 [1024, 512], P(None, 'grp'), may hold values from -0.1875 to 0.1875
- norm_gain: float32 [512], replicated, may hold values from 0.1 to 1.9
- norm_bias: float32 [512], replicated, may hold values from -3 to 3
- proj_weight: bfloat16 [512, 768], P(None, 'grp'), may hold values from -0.25 to 0.25
- proj_bias: float32 [768], replicated, may hold values from -3 to 3
- rec_length: int32 [4], P('grp'), may hold values from 8192 to 16384, as said below
- assign: int32 [3, 4, 16384], P(None, 'grp', 'rec'), may hold values from 0 to 999, as said below
- centroid_init: float32 [1024, 768], P('rec'), may hold values from -6 to 6
- prior_count: float32 [1024], P('rec'), may hold values from 50 to 500
Outputs:
- distortion: float32 [3, 4, 16384], P(None, 'grp', 'rec')
- centroids: float32 [1024, 768], P('rec')
Inputs may be any that keep to these rules, and one draw needn't show every extreme that they name: `rec_length`: some recording has all 16384 frames. `assign`: clusters form blocks of 8 consecutive ids (block b holds ids b * 8 to b * 8 + 7). In each iteration the 128 frames of one device name clusters of one block at most 2 times, and in each iteration some block is named exactly 2 times by the frames of every device of one recording.
All inputs are finite; a program needn't handle non-finite values.
Results may differ from a plain program's by a relative error of at most 0.0013.
Values may be sent and summed in bfloat16 or wider, within the bound.
A program may use at most 64 MiB of HBM per device.

v0:
```python
import jax
import jax.numpy as jnp
from jax import lax
from jax.sharding import PartitionSpec as P

K = 1000
ITERS = 3


def shifted(value, axis, steps):
    count = lax.axis_size(axis)
    initial, last = (max(0, -steps), min(count, count - steps))
    return lax.ppermute(value, axis, [(source, source + steps) for source in range(initial, last)])


def linear(inputs, weight):
    return jnp.dot(
        inputs,
        lax.all_gather(weight, "grp", axis=1, tiled=True),
        preferred_element_type=jnp.float32,
    )


def conv_layer(inputs, weight):
    return jax.nn.gelu(linear(inputs, weight), approximate=False).astype(jnp.bfloat16)


def shards(
    conv_in,
    conv5_weight,
    conv6_weight,
    conv7_weight,
    norm_gain,
    norm_bias,
    proj_weight,
    proj_bias,
    rec_length,
    assign,
    centroid_init,
    prior_count,
):
    signal = conv_in[0]
    sample_rows = signal.shape[0]
    channels = signal.shape[1]
    next_row = shifted(signal[:1], "rec", -1)
    paired = signal.reshape(sample_rows // 2, 2 * channels)
    trailing = jnp.concatenate([signal[2::2], next_row], 0)
    stacked = jnp.concatenate([paired, trailing], 1)
    hidden = conv_layer(stacked, conv5_weight)
    hidden = conv_layer(hidden.reshape(-1, 2 * channels), conv6_weight)
    hidden = conv_layer(hidden.reshape(-1, 2 * channels), conv7_weight)
    hidden_wide = hidden.astype(jnp.float32)
    average = jnp.mean(hidden_wide, axis=-1, keepdims=True)
    variance = jnp.mean((hidden_wide - average) ** 2, axis=-1, keepdims=True)
    normed = ((hidden_wide - average) * lax.rsqrt(variance + 1e-05) * norm_gain + norm_bias).astype(
        jnp.bfloat16
    )
    frames = (linear(normed, proj_weight) + proj_bias).astype(jnp.bfloat16)
    frame_count = frames.shape[0]
    feature_width = frames.shape[1]
    ranks_total = lax.axis_size("rec")
    slice_rows = centroid_init.shape[0]
    owners_used = (K + slice_rows - 1) // slice_rows
    capacity = max(2, (5 * frame_count + 4 * owners_used - 1) // (4 * owners_used))
    position = lax.axis_index("rec") * frame_count + jnp.arange(frame_count, dtype=jnp.int32)
    is_live = (position < rec_length[0]).astype(jnp.int32)
    frame_index = jnp.arange(frame_count, dtype=jnp.int32)
    earlier = (frame_index[None, :] < frame_index[:, None]).astype(jnp.bfloat16)
    owner_ids = jnp.arange(ranks_total, dtype=jnp.int32)
    cluster_ids = jnp.arange(slice_rows, dtype=jnp.int32)
    frames_wide = frames.astype(jnp.float32)
    centroid = centroid_init
    counts = prior_count
    results = []
    for iteration in range(ITERS):
        chosen = assign[iteration, 0]
        owner_id = chosen // slice_rows
        inner_id = chosen - owner_id * slice_rows
        owner_hot = (owner_id[:, None] == owner_ids[None, :]).astype(jnp.bfloat16)
        before = jnp.dot(earlier, owner_hot, preferred_element_type=jnp.float32)
        slot_id = jnp.sum(before * owner_hot.astype(jnp.float32), axis=1).astype(jnp.int32)
        target = owner_id * capacity + slot_id
        slot_total = ranks_total * capacity
        send_rows = jnp.zeros((slot_total, feature_width), jnp.bfloat16).at[target].set(frames)
        send_ids = jnp.full((slot_total,), -1, jnp.int32).at[target].set(inner_id)
        send_live = jnp.zeros((slot_total,), jnp.int32).at[target].set(is_live)
        got_rows, got_ids, got_live = (
            lax.all_to_all(
                send_rows.reshape(ranks_total, capacity, feature_width),
                "rec",
                split_axis=0,
                concat_axis=0,
                tiled=True,
            ),
            lax.all_to_all(
                send_ids.reshape(ranks_total, capacity),
                "rec",
                split_axis=0,
                concat_axis=0,
                tiled=True,
            ),
            lax.all_to_all(
                send_live.reshape(ranks_total, capacity),
                "rec",
                split_axis=0,
                concat_axis=0,
                tiled=True,
            ),
        )
        got_rows = got_rows.reshape(slot_total, feature_width)
        got_ids = got_ids.reshape(slot_total)
        got_live = got_live.reshape(slot_total)
        member = ((got_ids[:, None] == cluster_ids[None, :]) & (got_live[:, None] > 0)).astype(
            jnp.bfloat16
        )
        partial_value = jnp.dot(member.T, got_rows, preferred_element_type=jnp.float32)
        hit_count = jnp.sum(member.astype(jnp.float32), axis=0)
        coded = centroid.astype(jnp.bfloat16)
        codebook = lax.all_gather(coded, "rec", axis=0, tiled=True)
        picked = jnp.take(codebook, chosen, axis=0).astype(jnp.float32)
        gap_value = frames_wide - picked
        results.append(jnp.sum(gap_value * gap_value, axis=1) / feature_width)
        summed, hit_total = lax.psum((partial_value, hit_count), "grp")
        updated = counts + hit_total
        centroid = (counts[:, None] * centroid + summed) / updated[:, None]
        counts = updated
    distortion = jnp.stack(results, 0)[:, None, :]
    return (distortion, centroid)


def solution(mesh):
    in_specs = (
        P("grp", "rec", None),
        P(None, "grp"),
        P(None, "grp"),
        P(None, "grp"),
        P(),
        P(),
        P(None, "grp"),
        P(),
        P("grp"),
        P(None, "grp", "rec"),
        P("rec", None),
        P("rec"),
    )
    out_specs = (P(None, "grp", "rec"), P("rec", None))
    return jax.shard_map(shards, mesh=mesh, in_specs=in_specs, out_specs=out_specs, check_vma=False)
```

profile of v0, /device:TPU:1, one launch (start us, length us, event | category | flops | bytes accessed | tf_op | source)
XLA Modules:
  0.0 582.5 jit_solution(9825672385246203431)
XLA Ops:
  10.6 1.0 scatter_custom_fusion.3
  12.4 18.4 %all-to-all-start.3 = ((s32[128,1,2]{2,1,0:T(1,128)}), s32[128,1,2]{2,1,0:T(1,128)S(1)}, u32[]{:S(2)}, u32[]{:S(2)}) async-start(s32[128,1,2]{2,1,0:T(1,128)} %bitcast.16), calls=%async_computation.3 | async-start | bytes 131072 | tf_op jit(solution)/shard_map/all_to_all | solution.py:95
  31.6 2.8 collective-permute-start
  34.4 15.8 %all_gather.24 = bf16[512,768]{0,1:T(8,128)(2,1)S(1)} all-gather(bf16[512,192]{0,1:T(8,128)(2,1)} %param.20), channel_id=1, replica_groups=mesh['rec'=128,'grp'=4] {'grp'}, dimensions={1}, use_global_device_ids=true | all-gather | bytes 983040 | tf_op jit(solution)/shard_map/all_gather | solution.py:19
  51.3 1.0 scatter_custom_fusion.4
  52.3 1.0 scatter_custom_fusion.7
  53.3 1.0 scatter_custom_fusion.6
  56.5 1.2 slice.18
  57.7 1.0 scatter_custom_fusion.1
  58.7 1.0 scatter_custom_fusion
  61.2 4.9 fusion.12
  66.3 20.3 %all-gather.9.cloned.1.call-done = bf16[1024,512]{1,0:T(8,128)(2,1)} async-done(((bf16[1024,128]{1,0:T(8,128)(2,1)}), bf16[1024,512]{1,0:T(8,128)(2,1)}) %all-gather.9.cloned.1.call-update) | async-done | bytes 1048592 | tf_op jit(solution)/shard_map/all_gather | solution.py:19
  86.6 2.7 fusion.24
  89.4 15.9 %all-to-all-start.6 = ((s32[128,1,2]{2,1,0:T(1,128)}), s32[128,1,2]{2,1,0:T(1,128)S(1)}, u32[]{:S(2)}, u32[]{:S(2)}) async-start(s32[128,1,2]{2,1,0:T(1,128)} %bitcast.23), calls=%async_computation.6 | async-start | bytes 131072 | tf_op jit(solution)/shard_map/all_to_all | solution.py:95
  105.3 15.1 %all-gather.11.cloned.1.call-done = bf16[1024,512]{1,0:T(8,128)(2,1)} async-done(((bf16[1024,128]{1,0:T(8,128)(2,1)}), bf16[1024,512]{1,0:T(8,128)(2,1)}) %all-gather.11.cloned.1.call-update) | async-done | bytes 1048592 | tf_op jit(solution)/shard_map/all_gather | solution.py:19
  120.4 2.2 convert_reduce_fusion
  122.6 15.9 %all-to-all-start.4 = ((s32[128,1,2]{2,1,0:T(1,128)}), s32[128,1,2]{2,1,0:T(1,128)S(1)}, u32[]{:S(2)}, u32[]{:S(2)}) async-start(s32[128,1,2]{2,1,0:T(1,128)} %bitcast.17), calls=%async_computation.4 | async-start | bytes 131072 | tf_op jit(solution)/shard_map/all_to_all | solution.py:102
  138.5 11.5 %all-to-all-done.4 = s32[128,1,2]{2,1,0:T(1,128)S(1)} async-done(((s32[128,1,2]{2,1,0:T(1,128)}), s32[128,1,2]{2,1,0:T(1,128)S(1)}, u32[]{:S(2)}, u32[]{:S(2)}) %all-to-all-start.4) | async-done | bytes 1056 | tf_op jit(solution)/shard_map/all_to_all | solution.py:102
  150.1 5.6 all-to-all-start.7
  155.9 11.5 %all-to-all-done.7 = s32[128,1,2]{2,1,0:T(1,128)S(1)} async-done(((s32[128,1,2]{2,1,0:T(1,128)}), s32[128,1,2]{2,1,0:T(1,128)S(1)}, u32[]{:S(2)}, u32[]{:S(2)}) %all-to-all-start.7) | async-done | bytes 1056 | tf_op jit(solution)/shard_map/all_to_all | solution.py:102
  167.4 5.7 all-to-all-start
  173.1 11.7 %all-to-all-done = s32[128,1,2]{2,1,0:T(1,128)S(1)} async-done(((s32[128,1,2]{2,1,0:T(1,128)}), s32[128,1,2]{2,1,0:T(1,128)S(1)}, u32[]{:S(2)}, u32[]{:S(2)}) %all-to-all-start) | async-done | bytes 1056 | tf_op jit(solution)/shard_map/all_to_all | solution.py:95
  184.8 5.7 all-to-all-start.1
  190.9 1.2 scatter_custom_fusion.5
  192.1 0.9 reshape.450
  193.0 9.1 %all-to-all-done.1 = s32[128,1,2]{2,1,0:T(1,128)S(1)} async-done(((s32[128,1,2]{2,1,0:T(1,128)}), s32[128,1,2]{2,1,0:T(1,128)S(1)}, u32[]{:S(2)}, u32[]{:S(2)}) %all-to-all-start.1) | async-done | bytes 1056 | tf_op jit(solution)/shard_map/all_to_all | solution.py:102
  202.1 5.7 all-to-all-start.5
  207.8 1.2 scatter_custom_fusion.8
  209.1 0.9 reshape.452
  210.0 14.8 %all-to-all-done.5 = bf16[128,2,768]{2,1,0:T(2,128)(2,1)S(1)} async-done(((bf16[128,2,768]{2,1,0:T(2,128)(2,1)}), bf16[128,2,768]{2,1,0:T(2,128)(2,1)S(1)}, u32[]{:S(2)}, u32[]{:S(2)}) %all-to-all-start.5) | async-done | bytes 393248 | tf_op jit(solution)/shard_map/all_to_all | solution.py:88
  224.8 7.1 %all-to-all-start.8 = ((bf16[128,2,768]{2,1,0:T(2,128)(2,1)}), bf16[128,2,768]{2,1,0:T(2,128)(2,1)S(1)}, u32[]{:S(2)}, u32[]{:S(2)}) async-start(bf16[128,2,768]{2,1,0:T(2,128)(2,1)} %reshape.452), calls=%async_computation.8 | async-start | bytes 786432 | tf_op jit(solution)/shard_map/all_to_all | solution.py:88
  232.4 0.8 reduce.15
  233.3 0.8 reduce.17
  235.0 0.8 reduce.16
  236.0 1.2 scatter_custom_fusion.2
  237.2 0.9 reshape.448
  238.1 10.7 %all-to-all-done.8 = bf16[128,2,768]{2,1,0:T(2,128)(2,1)S(1)} async-done(((bf16[128,2,768]{2,1,0:T(2,128)(2,1)}), bf16[128,2,768]{2,1,0:T(2,128)(2,1)S(1)}, u32[]{:S(2)}, u32[]{:S(2)}) %all-to-all-start.8) | async-done | bytes 393248 | tf_op jit(solution)/shard_map/all_to_all | solution.py:88
  248.8 7.1 %all-to-all-start.2 = ((bf16[128,2,768]{2,1,0:T(2,128)(2,1)}), bf16[128,2,768]{2,1,0:T(2,128)(2,1)S(1)}, u32[]{:S(2)}, u32[]{:S(2)}) async-start(bf16[128,2,768]{2,1,0:T(2,128)(2,1)} %reshape.448), calls=%async_computation.2 | async-start | bytes 786432 | tf_op jit(solution)/shard_map/all_to_all | solution.py:88
  259.6 13.2 %all-to-all-done.2 = bf16[128,2,768]{2,1,0:T(2,128)(2,1)S(1)} async-done(((bf16[128,2,768]{2,1,0:T(2,128)(2,1)}), bf16[128,2,768]{2,1,0:T(2,128)(2,1)S(1)}, u32[]{:S(2)}, u32[]{:S(2)}) %all-to-all-start.2) | async-done | bytes 393248 | tf_op jit(solution)/shard_map/all_to_all | solution.py:88
  272.9 0.8 fusion.73
  273.8 42.7 %all-reduce.3.cloned.1.call-done = (f32[8]{0:T(128)}, f32[8,768]{1,0:T(8,128)}, f32[8,768]{1,0:T(8,128)}, f32[8]{0:T(128)}, f32[8,768]{1,0:T(8,128)}, /*index=5*/f32[8]{0:T(128)}) async-done(((f32[8]{0:T(128)}, f32[8,768]{1,0:T(8,128)}, f32[8,768]{1,0:T(8,128)}, f32[8]{0:T(128)}, f32[8,768]{1,0:T(8,128)}, /*index=5*/f32[8]{0:T(128)}), (f32[8]{0:T(128)}, f32[8,768]{1,0:T(8,128)}, f32[8,768]{1,0:T(8,128)}, ...) | async-done | bytes 73840 | tf_op jit(solution)/shard_map/psum | solution.py:123
  317.2 1.5 add_divide_fusion
  320.0 85.9 %all-gather.15.cloned.1.call-done = bf16[1024,768]{1,0:T(8,128)(2,1)} async-done(((bf16[8,768]{1,0:T(8,128)(2,1)}), bf16[1024,768]{1,0:T(8,128)(2,1)}) %all-gather.15.cloned.1.call-update) | async-done | bytes 1572880 | tf_op jit(solution)/shard_map/all_gather | solution.py:119
  405.9 2.6 gather_fusion.1
  408.5 80.4 %all-gather.17.cloned.1.call-done = bf16[1024,768]{1,0:T(8,128)(2,1)} async-done(((bf16[8,768]{1,0:T(8,128)(2,1)}), bf16[1024,768]{1,0:T(8,128)(2,1)}) %all-gather.17.cloned.1.call-update) | async-done | bytes 1572880 | tf_op jit(solution)/shard_map/all_gather | solution.py:119
  488.9 2.6 gather_fusion.2
  491.5 80.6 %all-gather.13.cloned.1.call-done = bf16[1024,768]{1,0:T(8,128)(2,1)} async-done(((bf16[8,768]{1,0:T(8,128)(2,1)}), bf16[1024,768]{1,0:T(8,128)(2,1)}) %all-gather.13.cloned.1.call-update) | async-done | bytes 1572880 | tf_op jit(solution)/shard_map/all_gather | solution.py:119
  572.1 2.6 gather_fusion
  (79 shorter events, 18.5 us)
Async XLA Ops:
  7.2 43.7 %copy-start = (bf16[1,1024,512]{2,1,0:T(8,128)(2,1)S(1)}, bf16[1,1024,512]{2,1,0:T(8,128)(2,1)}, u32[]{:S(2)}) copy-start(bf16[1,1024,512]{2,1,0:T(8,128)(2,1)} %param.14) | copy-start | bytes 3145732
  7.2 54.0 %all-gather.7.cloned.1.call-start = ((), (), s32[]{:S(2)}) async-start(), calls=%async_computation.9 | async-start | bytes 1966080 | tf_op jit(solution)/shard_map/all_gather | solution.py:19
  7.9 78.7 %all-gather.9.cloned.1.call-start = ((), (), s32[]{:S(2)}) async-start(), calls=%async_computation.10 | async-start | bytes 1310720 | tf_op jit(solution)/shard_map/all_gather | solution.py:19
  12.4 77.0 %all-to-all-start.3 = ((s32[128,1,2]{2,1,0:T(1,128)}), s32[128,1,2]{2,1,0:T(1,128)S(1)}, u32[]{:S(2)}, u32[]{:S(2)}) async-start(s32[128,1,2]{2,1,0:T(1,128)} %bitcast.16), calls=%async_computation.3 | async-start | bytes 131072 | tf_op jit(solution)/shard_map/all_to_all | solution.py:95
  30.8 89.6 %all-gather.11.cloned.1.call-start = ((), (), s32[]{:S(2)}) async-start(), calls=%async_computation.11 | async-start | bytes 1310720 | tf_op jit(solution)/shard_map/all_gather | solution.py:19
  31.6 29.6 %collective-permute-start = (bf16[1,512]{1,0:T(2,128)(2,1)S(1)}, bf16[1,512]{1,0:T(2,128)(2,1)S(1)}, u32[]{:S(2)}, u32[]{:S(2)}) collective-permute-start(bf16[1,512]{1,0:T(2,128)(2,1)S(1)} %slice_bitcast_fusion), channel_id=1, source_target_pairs={{4,0},{8,4},{12,8},{16,12},{20,16},{24,20},{28,24},{32,28},{36,32}... | collective-permute-start | bytes 3080 | tf_op jit(solution)/shard_map/ppermute | solution.py:13
  89.4 33.2 %all-to-all-start.6 = ((s32[128,1,2]{2,1,0:T(1,128)}), s32[128,1,2]{2,1,0:T(1,128)S(1)}, u32[]{:S(2)}, u32[]{:S(2)}) async-start(s32[128,1,2]{2,1,0:T(1,128)} %bitcast.23), calls=%async_computation.6 | async-start | bytes 131072 | tf_op jit(solution)/shard_map/all_to_all | solution.py:95
  105.3 85.1 %copy-start.4 = (f32[768]{0:T(1024)S(1)}, f32[768]{0:T(1024)}, u32[]{:S(2)}) copy-start(f32[768]{0:T(1024)} %param.21) | copy-start | bytes 9220
  105.3 85.1 %copy-start.5 = (f32[512]{0:T(512)S(1)}, f32[512]{0:T(512)}, u32[]{:S(2)}) copy-start(f32[512]{0:T(512)} %param.19) | copy-start | bytes 6148
  105.3 85.1 %copy-start.6 = (f32[512]{0:T(512)S(1)}, f32[512]{0:T(512)}, u32[]{:S(2)}) copy-start(f32[512]{0:T(512)} %param.18) | copy-start | bytes 6148
  122.6 27.4 %all-to-all-start.4 = ((s32[128,1,2]{2,1,0:T(1,128)}), s32[128,1,2]{2,1,0:T(1,128)S(1)}, u32[]{:S(2)}, u32[]{:S(2)}) async-start(s32[128,1,2]{2,1,0:T(1,128)} %bitcast.17), calls=%async_computation.4 | async-start | bytes 131072 | tf_op jit(solution)/shard_map/all_to_all | solution.py:102
  150.1 17.3 %all-to-all-start.7 = ((s32[128,1,2]{2,1,0:T(1,128)}), s32[128,1,2]{2,1,0:T(1,128)S(1)}, u32[]{:S(2)}, u32[]{:S(2)}) async-start(s32[128,1,2]{2,1,0:T(1,128)} %bitcast.24), calls=%async_computation.7 | async-start | bytes 131072 | tf_op jit(solution)/shard_map/all_to_all | solution.py:102
  167.4 17.4 %all-to-all-start = ((s32[128,1,2]{2,1,0:T(1,128)}), s32[128,1,2]{2,1,0:T(1,128)S(1)}, u32[]{:S(2)}, u32[]{:S(2)}) async-start(s32[128,1,2]{2,1,0:T(1,128)} %bitcast.8), calls=%async_computation | async-start | bytes 131072 | tf_op jit(solution)/shard_map/all_to_all | solution.py:95
  184.8 17.3 %all-to-all-start.1 = ((s32[128,1,2]{2,1,0:T(1,128)}), s32[128,1,2]{2,1,0:T(1,128)S(1)}, u32[]{:S(2)}, u32[]{:S(2)}) async-start(s32[128,1,2]{2,1,0:T(1,128)} %bitcast.10), calls=%async_computation.1 | async-start | bytes 131072 | tf_op jit(solution)/shard_map/all_to_all | solution.py:102
  202.1 22.6 %all-to-all-start.5 = ((bf16[128,2,768]{2,1,0:T(2,128)(2,1)}), bf16[128,2,768]{2,1,0:T(2,128)(2,1)S(1)}, u32[]{:S(2)}, u32[]{:S(2)}) async-start(bf16[128,2,768]{2,1,0:T(2,128)(2,1)} %reshape.450), calls=%async_computation.5 | async-start | bytes 786432 | tf_op jit(solution)/shard_map/all_to_all | solution.py:88
  224.8 24.0 %all-to-all-start.8 = ((bf16[128,2,768]{2,1,0:T(2,128)(2,1)}), bf16[128,2,768]{2,1,0:T(2,128)(2,1)S(1)}, u32[]{:S(2)}, u32[]{:S(2)}) async-start(bf16[128,2,768]{2,1,0:T(2,128)(2,1)} %reshape.452), calls=%async_computation.8 | async-start | bytes 786432 | tf_op jit(solution)/shard_map/all_to_all | solution.py:88
  248.8 24.0 %all-to-all-start.2 = ((bf16[128,2,768]{2,1,0:T(2,128)(2,1)}), bf16[128,2,768]{2,1,0:T(2,128)(2,1)S(1)}, u32[]{:S(2)}, u32[]{:S(2)}) async-start(bf16[128,2,768]{2,1,0:T(2,128)(2,1)} %reshape.448), calls=%async_computation.2 | async-start | bytes 786432 | tf_op jit(solution)/shard_map/all_to_all | solution.py:88
  255.9 60.6 %all-reduce.3.cloned.1.call-start = ((), (), s32[]{:S(2)}) async-start(), calls=%async_computation.15 | async-start | bytes 150528 | tf_op jit(solution)/shard_map/psum | solution.py:123
  257.8 58.7 %copy-start.3 = (f32[8]{0:T(128)S(1)}, f32[8]{0:T(128)}, u32[]{:S(2)}) copy-start(f32[8]{0:T(128)} %param.25) | copy-start | bytes 100
  257.8 59.3 %copy-start.1 = (f32[8,768]{1,0:T(8,128)S(1)}, f32[8,768]{1,0:T(8,128)}, u32[]{:S(2)}) copy-start(f32[8,768]{1,0:T(8,128)} %param.24) | copy-start | bytes 73732
  257.8 62.1 %copy-start.2 = (s32[3,1,128]{2,1,0:T(1,128)S(1)}, s32[3,1,128]{2,1,0:T(1,128)}, u32[]{:S(2)}) copy-start(s32[3,1,128]{2,1,0:T(1,128)} %param.23) | copy-start | bytes 4612
  273.8 132.2 %all-gather.15.cloned.1.call-start = ((), (), s32[]{:S(2)}) async-start(), calls=%async_computation.13 | async-start | bytes 1585152 | tf_op jit(solution)/shard_map/all_gather | solution.py:119
  318.7 170.3 %all-gather.17.cloned.1.call-start = ((), (), s32[]{:S(2)}) async-start(), calls=%async_computation.14 | async-start | bytes 1585152 | tf_op jit(solution)/shard_map/all_gather | solution.py:119
  319.2 252.9 %all-gather.13.cloned.1.call-start = ((), (), s32[]{:S(2)}) async-start(), calls=%async_computation.12 | async-start | bytes 1585152 | tf_op jit(solution)/shard_map/all_gather | solution.py:119
Sparse Core Ops, SparseCore 0:
  10.1 43.5 all-gather.6
  55.7 30.8 all-gather.8
  88.7 31.7 all-gather.10
  273.9 42.5 all-reduce.2
  319.5 86.3 all-gather.14
  409.0 79.8 all-gather.16
  492.1 79.9 all-gather.12
where the time goes:
time: 583 us; the launch traced here: 582 us
  waiting for transfers between devices  410 us (70%)
  starting transfers between devices  90.2 us (15%)
  local copies, waits for them, and re-layouts  29.5 us (5%)
  blocking collectives  15.8 us (3%)
  between operations  15.3 us (3%)
  matrix products  13.1 us (2%)
  other arithmetic  8.61 us (1%)
    all_gather x3, waiting for transfers between devices, shards(): codebook = lax.all_gather(coded, 'rec', axis=0, tiled=True)  247 us
    psum x1, waiting for transfers between devices, shards(): summed, hit_total = lax.psum((partial_value, hit_count), 'grp')  42.7 us
    all_to_all x3, starting transfers between devices, shards(): lax.all_to_all(send_ids.reshape(ranks_total, capacity), 'rec', split_axis...  40 us
    all_to_all x3, waiting for transfers between devices, shards(): lax.all_to_all(send_rows.reshape(ranks_total, capacity, feature_width), '...  38.6 us
    all_gather x3, waiting for transfers between devices, linear(): lax.all_gather(weight, 'grp', axis=1, tiled=True)  35.4 us
    all_to_all x3, waiting for transfers between devices, shards(): lax.all_to_all(send_live.reshape(ranks_total, capacity), 'rec', split_axi...  32.1 us
    all_to_all x3, starting transfers between devices, shards(): lax.all_to_all(send_live.reshape(ranks_total, capacity), 'rec', split_axi...  27.2 us
    all_to_all x3, starting transfers between devices, shards(): lax.all_to_all(send_rows.reshape(ranks_total, capacity, feature_width), '...  19.9 us
  transfers between devices with their start and end apart: 17, of which 13 were waited for; matrix products, arithmetic and copies ran while one was open for 7% of the time, Pallas kernels for 0%

commit v1 on v0

--- a/solution.py
+++ b/solution.py
@@ -116,7 +116,10 @@
         partial_value = jnp.dot(member.T, got_rows, preferred_element_type=jnp.float32)
         hit_count = jnp.sum(member.astype(jnp.float32), axis=0)
         coded = centroid.astype(jnp.bfloat16)
-        codebook = lax.all_gather(coded, "rec", axis=0, tiled=True)
+        size = lax.axis_size("rec")
+        blocks = jnp.stack([coded for _ in range(size)])
+        blocks = lax.all_to_all(blocks, "rec", split_axis=0, concat_axis=0)
+        codebook = jnp.concatenate(blocks, axis=0)
         picked = jnp.take(codebook, chosen, axis=0).astype(jnp.float32)
         gap_value = frames_wide - picked
         results.append(jnp.sum(gap_value * gap_value, axis=1) / feature_width)

time: 583 us -> 493 us (0.85); the launches traced: 582 us -> 484 us
  waiting for transfers between devices: 410 us -> 199 us
  blocking collectives: 15.8 us -> 122 us
  starting transfers between devices: 90.2 us -> 98.6 us
    all_gather x3 -> x0, waiting for transfers between devices: 247 us -> none  [shards(): codebook = lax.all_gather(coded, 'rec', axis=0, tiled=True)]
    all_to_all x0 -> x2, blocking collectives: none -> 106 us  [shards(): blocks = lax.all_to_all(blocks, 'rec', split_axis=0, concat_axis=0)]
    all_to_all x0 -> x1, waiting for transfers between devices: none -> 37.6 us  [shards(): blocks = lax.all_to_all(blocks, 'rec', split_axis=0, concat_axis=0)]
    all_to_all x0 -> x1, starting transfers between devices: none -> 7.71 us  [shards(): blocks = lax.all_to_all(blocks, 'rec', split_axis=0, concat_axis=0)]
  transfers between devices with their start and end apart: 17 -> 15, of which waited for: 13 -> 11; matrix products, arithmetic and copies ran while one was open for 7% -> 8% of each run, Pallas kernels for 0% -> 0%
where the time goes in v1:
time: 493 us; the launch traced here: 484 us
  waiting for transfers between devices  199 us (40%)
  blocking collectives  122 us (25%)
  starting transfers between devices  98.6 us (20%)
  local copies, waits for them, and re-layouts  27.6 us (6%)
  between operations  15.2 us (3%)
  matrix products  13.1 us (3%)
  other arithmetic  8.61 us (2%)
    all_to_all x2, blocking collectives, shards(): blocks = lax.all_to_all(blocks, 'rec', split_axis=0, concat_axis=0)  106 us
    psum x1, waiting for transfers between devices, shards(): summed, hit_total = lax.psum((partial_value, hit_count), 'grp')  42.7 us
    all_to_all x3, starting transfers between devices, shards(): lax.all_to_all(send_ids.reshape(ranks_total, capacity), 'rec', split_axis...  40.6 us
    all_to_all x3, waiting for transfers between devices, shards(): lax.all_to_all(send_rows.reshape(ranks_total, capacity, feature_width), '...  38.5 us
    all_to_all x1, waiting for transfers between devices, shards(): blocks = lax.all_to_all(blocks, 'rec', split_axis=0, concat_axis=0)  37.6 us
    all_gather x3, waiting for transfers between devices, linear(): lax.all_gather(weight, 'grp', axis=1, tiled=True)  34.8 us
    all_to_all x3, waiting for transfers between devices, shards(): lax.all_to_all(send_live.reshape(ranks_total, capacity), 'rec', split_axi...  32.1 us
    all_to_all x3, starting transfers between devices, shards(): lax.all_to_all(send_live.reshape(ranks_total, capacity), 'rec', split_axi...  27.2 us
  transfers between devices with their start and end apart: 15, of which 11 were waited for; matrix products, arithmetic and copies ran while one was open for 8% of the time, Pallas kernels for 0%

profile of v1, /device:TPU:1, one launch (start us, length us, event | category | flops | bytes accessed | tf_op | source)
XLA Modules:
  0.0 483.6 jit_solution(5708602719484677502)
XLA Ops:
  10.6 1.0 scatter_custom_fusion.3
  12.4 18.4 %all-to-all-start.5 = ((s32[128,1,2]{2,1,0:T(1,128)}), s32[128,1,2]{2,1,0:T(1,128)S(1)}, u32[]{:S(2)}, u32[]{:S(2)}) async-start(s32[128,1,2]{2,1,0:T(1,128)} %bitcast.18), calls=%async_computation.5 | async-start | bytes 131072 | tf_op jit(solution)/shard_map/all_to_all | solution.py:95
  31.6 2.8 collective-permute-start
  34.4 15.8 %all_gather.15 = bf16[512,768]{0,1:T(8,128)(2,1)S(1)} all-gather(bf16[512,192]{0,1:T(8,128)(2,1)} %param.20), channel_id=1, replica_groups=mesh['rec'=128,'grp'=4] {'grp'}, dimensions={1}, use_global_device_ids=true | all-gather | bytes 983040 | tf_op jit(solution)/shard_map/all_gather | solution.py:19
  51.3 1.0 scatter_custom_fusion.4
  52.3 1.0 scatter_custom_fusion.7
  53.3 1.0 scatter_custom_fusion.6
  56.5 1.2 slice.18
  57.7 1.0 scatter_custom_fusion.1
  58.7 1.0 scatter_custom_fusion
  61.2 4.9 %fusion.12 = bf16[512,512]{1,0:T(8,128)(2,1)S(1)} fusion(bf16[1536,512]{1,0:T(8,128)(2,1)} %all-gather.4.cloned.1.call-done, bf16[1,512]{1,0:T(2,128)(2,1)S(1)} %collective-permute-done, bf16[511,512]{1,0:T(8,128)(2,1)S(1)} %slice.18, bf16[512,1024]{1,0:T(8,128)(2,1)S(1)} %reshape_squeeze.3), kind=kOutput, calls=%fused_computation.29 | convolution fusion | flops 827064320 | bytes 3670016 | tf_op jit(solution)/shard_map/dot_general | solution.py:17
  66.3 20.3 %all-gather.6.cloned.1.call-done = bf16[1024,512]{1,0:T(8,128)(2,1)} async-done(((bf16[1024,128]{1,0:T(8,128)(2,1)}), bf16[1024,512]{1,0:T(8,128)(2,1)}) %all-gather.6.cloned.1.call-update) | async-done | bytes 1048592 | tf_op jit(solution)/shard_map/all_gather | solution.py:19
  86.6 2.7 fusion.24
  89.4 16.5 %all-to-all-start.9 = ((s32[128,1,2]{2,1,0:T(1,128)}), s32[128,1,2]{2,1,0:T(1,128)S(1)}, u32[]{:S(2)}, u32[]{:S(2)}) async-start(s32[128,1,2]{2,1,0:T(1,128)} %bitcast.26), calls=%async_computation.9 | async-start | bytes 131072 | tf_op jit(solution)/shard_map/all_to_all | solution.py:95
  105.9 14.5 %all-gather.8.cloned.1.call-done = bf16[1024,512]{1,0:T(8,128)(2,1)} async-done(((bf16[1024,128]{1,0:T(8,128)(2,1)}), bf16[1024,512]{1,0:T(8,128)(2,1)}) %all-gather.8.cloned.1.call-update) | async-done | bytes 1048592 | tf_op jit(solution)/shard_map/all_gather | solution.py:19
  120.4 2.2 convert_reduce_fusion
  122.6 15.9 %all-to-all-start.6 = ((s32[128,1,2]{2,1,0:T(1,128)}), s32[128,1,2]{2,1,0:T(1,128)S(1)}, u32[]{:S(2)}, u32[]{:S(2)}) async-start(s32[128,1,2]{2,1,0:T(1,128)} %bitcast.19), calls=%async_computation.6 | async-start | bytes 131072 | tf_op jit(solution)/shard_map/all_to_all | solution.py:102
  138.5 11.5 %all-to-all-done.6 = s32[128,1,2]{2,1,0:T(1,128)S(1)} async-done(((s32[128,1,2]{2,1,0:T(1,128)}), s32[128,1,2]{2,1,0:T(1,128)S(1)}, u32[]{:S(2)}, u32[]{:S(2)}) %all-to-all-start.6) | async-done | bytes 1056 | tf_op jit(solution)/shard_map/all_to_all | solution.py:102
  150.1 5.6 %all-to-all-start.10 = ((s32[128,1,2]{2,1,0:T(1,128)}), s32[128,1,2]{2,1,0:T(1,128)S(1)}, u32[]{:S(2)}, u32[]{:S(2)}) async-start(s32[128,1,2]{2,1,0:T(1,128)} %bitcast.27), calls=%async_computation.10 | async-start | bytes 131072 | tf_op jit(solution)/shard_map/all_to_all | solution.py:102
  155.9 11.5 %all-to-all-done.10 = s32[128,1,2]{2,1,0:T(1,128)S(1)} async-done(((s32[128,1,2]{2,1,0:T(1,128)}), s32[128,1,2]{2,1,0:T(1,128)S(1)}, u32[]{:S(2)}, u32[]{:S(2)}) %all-to-all-start.10) | async-done | bytes 1056 | tf_op jit(solution)/shard_map/all_to_all | solution.py:102
  167.4 5.7 %all-to-all-start.1 = ((s32[128,1,2]{2,1,0:T(1,128)}), s32[128,1,2]{2,1,0:T(1,128)S(1)}, u32[]{:S(2)}, u32[]{:S(2)}) async-start(s32[128,1,2]{2,1,0:T(1,128)} %bitcast.9), calls=%async_computation.1 | async-start | bytes 131072 | tf_op jit(solution)/shard_map/all_to_all | solution.py:95
  173.1 11.7 %all-to-all-done.1 = s32[128,1,2]{2,1,0:T(1,128)S(1)} async-done(((s32[128,1,2]{2,1,0:T(1,128)}), s32[128,1,2]{2,1,0:T(1,128)S(1)}, u32[]{:S(2)}, u32[]{:S(2)}) %all-to-all-start.1) | async-done | bytes 1056 | tf_op jit(solution)/shard_map/all_to_all | solution.py:95
  184.8 5.7 %all-to-all-start.2 = ((s32[128,1,2]{2,1,0:T(1,128)}), s32[128,1,2]{2,1,0:T(1,128)S(1)}, u32[]{:S(2)}, u32[]{:S(2)}) async-start(s32[128,1,2]{2,1,0:T(1,128)} %bitcast.11), calls=%async_computation.2 | async-start | bytes 131072 | tf_op jit(solution)/shard_map/all_to_all | solution.py:102
  190.9 1.2 scatter_custom_fusion.5
  192.2 0.9 reshape.467
  193.0 9.1 %all-to-all-done.2 = s32[128,1,2]{2,1,0:T(1,128)S(1)} async-done(((s32[128,1,2]{2,1,0:T(1,128)}), s32[128,1,2]{2,1,0:T(1,128)S(1)}, u32[]{:S(2)}, u32[]{:S(2)}) %all-to-all-start.2) | async-done | bytes 1056 | tf_op jit(solution)/shard_map/all_to_all | solution.py:102
  202.1 6.0 %all-to-all-start.7 = ((bf16[128,2,768]{2,1,0:T(2,128)(2,1)}), bf16[128,2,768]{2,1,0:T(2,128)(2,1)S(1)}, u32[]{:S(2)}, u32[]{:S(2)}) async-start(bf16[128,2,768]{2,1,0:T(2,128)(2,1)} %reshape.467), calls=%async_computation.7 | async-start | bytes 786432 | tf_op jit(solution)/shard_map/all_to_all | solution.py:88
  208.1 1.2 scatter_custom_fusion.8
  209.4 0.9 reshape.470
  210.3 14.7 %all-to-all-done.7 = bf16[128,2,768]{2,1,0:T(2,128)(2,1)S(1)} async-done(((bf16[128,2,768]{2,1,0:T(2,128)(2,1)}), bf16[128,2,768]{2,1,0:T(2,128)(2,1)S(1)}, u32[]{:S(2)}, u32[]{:S(2)}) %all-to-all-start.7) | async-done | bytes 393248 | tf_op jit(solution)/shard_map/all_to_all | solution.py:88
  224.9 7.1 %all-to-all-start.11 = ((bf16[128,2,768]{2,1,0:T(2,128)(2,1)}), bf16[128,2,768]{2,1,0:T(2,128)(2,1)S(1)}, u32[]{:S(2)}, u32[]{:S(2)}) async-start(bf16[128,2,768]{2,1,0:T(2,128)(2,1)} %reshape.470), calls=%async_computation.11 | async-start | bytes 786432 | tf_op jit(solution)/shard_map/all_to_all | solution.py:88
  233.5 0.8 reduce.17
  235.2 0.8 reduce.16
  236.2 1.2 scatter_custom_fusion.2
  237.4 0.9 reshape.464
  238.3 10.7 %all-to-all-done.11 = bf16[128,2,768]{2,1,0:T(2,128)(2,1)S(1)} async-done(((bf16[128,2,768]{2,1,0:T(2,128)(2,1)}), bf16[128,2,768]{2,1,0:T(2,128)(2,1)S(1)}, u32[]{:S(2)}, u32[]{:S(2)}) %all-to-all-start.11) | async-done | bytes 393248 | tf_op jit(solution)/shard_map/all_to_all | solution.py:88
  248.9 7.1 %all-to-all-start.3 = ((bf16[128,2,768]{2,1,0:T(2,128)(2,1)}), bf16[128,2,768]{2,1,0:T(2,128)(2,1)S(1)}, u32[]{:S(2)}, u32[]{:S(2)}) async-start(bf16[128,2,768]{2,1,0:T(2,128)(2,1)} %reshape.464), calls=%async_computation.3 | async-start | bytes 786432 | tf_op jit(solution)/shard_map/all_to_all | solution.py:88
  259.7 13.2 %all-to-all-done.3 = bf16[128,2,768]{2,1,0:T(2,128)(2,1)S(1)} async-done(((bf16[128,2,768]{2,1,0:T(2,128)(2,1)}), bf16[128,2,768]{2,1,0:T(2,128)(2,1)S(1)}, u32[]{:S(2)}, u32[]{:S(2)}) %all-to-all-start.3) | async-done | bytes 393248 | tf_op jit(solution)/shard_map/all_to_all | solution.py:88
  273.9 42.7 %all-reduce.3.cloned.1.call-done = (f32[8]{0:T(128)}, f32[8,768]{1,0:T(8,128)}, f32[8,768]{1,0:T(8,128)}, f32[8]{0:T(128)}, f32[8,768]{1,0:T(8,128)}, /*index=5*/f32[8]{0:T(128)}) async-done(((f32[8]{0:T(128)}, f32[8,768]{1,0:T(8,128)}, f32[8,768]{1,0:T(8,128)}, f32[8]{0:T(128)}, f32[8,768]{1,0:T(8,128)}, /*index=5*/f32[8]{0:T(128)}), (f32[8]{0:T(128)}, f32[8,768]{1,0:T(8,128)}, f32[8,768]{1,0:T(8,128)}, ...) | async-done | bytes 73840 | tf_op jit(solution)/shard_map/psum | solution.py:126
  317.3 1.5 add_divide_fusion
  318.9 57.2 %all_to_all.84 = bf16[128,8,768]{2,1,0:T(8,128)(2,1)S(1)} all-to-all(bf16[128,8,768]{2,1,0:T(8,128)(2,1)S(1)} %stack.9), channel_id=1, replica_groups=mesh['rec'=128,'grp'=4] {'rec'}, dimensions={0} | all-to-all | bytes 3145728 | tf_op jit(solution)/shard_map/all_to_all | solution.py:121
  376.2 48.6 %all_to_all.85 = bf16[128,8,768]{2,1,0:T(8,128)(2,1)} all-to-all(bf16[128,8,768]{2,1,0:T(8,128)(2,1)S(1)} %stack.10), channel_id=1, replica_groups=mesh['rec'=128,'grp'=4] {'rec'}, dimensions={0} | all-to-all | bytes 3145728 | tf_op jit(solution)/shard_map/all_to_all | solution.py:121
  424.8 1.3 stack.8
  426.1 7.7 %all-to-all-start = ((bf16[128,8,768]{2,1,0:T(8,128)(2,1)}), bf16[128,8,768]{2,1,0:T(8,128)(2,1)S(1)}, u32[]{:S(2)}, u32[]{:S(2)}) async-start(bf16[128,8,768]{2,1,0:T(8,128)(2,1)} %stack.8), calls=%async_computation | async-start | bytes 3145728 | tf_op jit(solution)/shard_map/all_to_all | solution.py:121
  433.9 0.9 gather_fusion.1
  434.7 2.6 gather_fusion.2
  437.4 37.6 %all-to-all-done = bf16[128,8,768]{2,1,0:T(8,128)(2,1)S(1)} async-done(((bf16[128,8,768]{2,1,0:T(8,128)(2,1)}), bf16[128,8,768]{2,1,0:T(8,128)(2,1)S(1)}, u32[]{:S(2)}, u32[]{:S(2)}) %all-to-all-start) | async-done | bytes 1572896 | tf_op jit(solution)/shard_map/all_to_all | solution.py:121
  474.9 0.9 gather_fusion
  (81 shorter events, 18.9 us)
Async XLA Ops:
  7.2 43.7 %copy-start = (bf16[1,1024,512]{2,1,0:T(8,128)(2,1)S(1)}, bf16[1,1024,512]{2,1,0:T(8,128)(2,1)}, u32[]{:S(2)}) copy-start(bf16[1,1024,512]{2,1,0:T(8,128)(2,1)} %param.14) | copy-start | bytes 3145732
  7.2 54.0 %all-gather.4.cloned.1.call-start = ((), (), s32[]{:S(2)}) async-start(), calls=%async_computation.12 | async-start | bytes 1966080 | tf_op jit(solution)/shard_map/all_gather | solution.py:19
  7.9 78.7 %all-gather.6.cloned.1.call-start = ((), (), s32[]{:S(2)}) async-start(), calls=%async_computation.13 | async-start | bytes 1310720 | tf_op jit(solution)/shard_map/all_gather | solution.py:19
  12.4 77.0 %all-to-all-start.5 = ((s32[128,1,2]{2,1,0:T(1,128)}), s32[128,1,2]{2,1,0:T(1,128)S(1)}, u32[]{:S(2)}, u32[]{:S(2)}) async-start(s32[128,1,2]{2,1,0:T(1,128)} %bitcast.18), calls=%async_computation.5 | async-start | bytes 131072 | tf_op jit(solution)/shard_map/all_to_all | solution.py:95
  30.8 89.6 %all-gather.8.cloned.1.call-start = ((), (), s32[]{:S(2)}) async-start(), calls=%async_computation.14 | async-start | bytes 1310720 | tf_op jit(solution)/shard_map/all_gather | solution.py:19
  31.6 29.6 %collective-permute-start = (bf16[1,512]{1,0:T(2,128)(2,1)S(1)}, bf16[1,512]{1,0:T(2,128)(2,1)S(1)}, u32[]{:S(2)}, u32[]{:S(2)}) collective-permute-start(bf16[1,512]{1,0:T(2,128)(2,1)S(1)} %slice_bitcast_fusion), channel_id=1, source_target_pairs={{4,0},{8,4},{12,8},{16,12},{20,16},{24,20},{28,24},{32,28},{36,32}... | collective-permute-start | bytes 3080 | tf_op jit(solution)/shard_map/ppermute | solution.py:13
  89.4 33.2 %all-to-all-start.9 = ((s32[128,1,2]{2,1,0:T(1,128)}), s32[128,1,2]{2,1,0:T(1,128)S(1)}, u32[]{:S(2)}, u32[]{:S(2)}) async-start(s32[128,1,2]{2,1,0:T(1,128)} %bitcast.26), calls=%async_computation.9 | async-start | bytes 131072 | tf_op jit(solution)/shard_map/all_to_all | solution.py:95
  105.9 84.6 %copy-start.6 = (f32[768]{0:T(1024)S(1)}, f32[768]{0:T(1024)}, u32[]{:S(2)}) copy-start(f32[768]{0:T(1024)} %param.21) | copy-start | bytes 9220
  105.9 84.6 %copy-start.7 = (f32[512]{0:T(512)S(1)}, f32[512]{0:T(512)}, u32[]{:S(2)}) copy-start(f32[512]{0:T(512)} %param.19) | copy-start | bytes 6148
  105.9 84.6 %copy-start.8 = (f32[512]{0:T(512)S(1)}, f32[512]{0:T(512)}, u32[]{:S(2)}) copy-start(f32[512]{0:T(512)} %param.18) | copy-start | bytes 6148
  122.6 27.4 %all-to-all-start.6 = ((s32[128,1,2]{2,1,0:T(1,128)}), s32[128,1,2]{2,1,0:T(1,128)S(1)}, u32[]{:S(2)}, u32[]{:S(2)}) async-start(s32[128,1,2]{2,1,0:T(1,128)} %bitcast.19), calls=%async_computation.6 | async-start | bytes 131072 | tf_op jit(solution)/shard_map/all_to_all | solution.py:102
  150.1 17.3 %all-to-all-start.10 = ((s32[128,1,2]{2,1,0:T(1,128)}), s32[128,1,2]{2,1,0:T(1,128)S(1)}, u32[]{:S(2)}, u32[]{:S(2)}) async-start(s32[128,1,2]{2,1,0:T(1,128)} %bitcast.27), calls=%async_computation.10 | async-start | bytes 131072 | tf_op jit(solution)/shard_map/all_to_all | solution.py:102
  167.4 17.4 %all-to-all-start.1 = ((s32[128,1,2]{2,1,0:T(1,128)}), s32[128,1,2]{2,1,0:T(1,128)S(1)}, u32[]{:S(2)}, u32[]{:S(2)}) async-start(s32[128,1,2]{2,1,0:T(1,128)} %bitcast.9), calls=%async_computation.1 | async-start | bytes 131072 | tf_op jit(solution)/shard_map/all_to_all | solution.py:95
  184.8 17.3 %all-to-all-start.2 = ((s32[128,1,2]{2,1,0:T(1,128)}), s32[128,1,2]{2,1,0:T(1,128)S(1)}, u32[]{:S(2)}, u32[]{:S(2)}) async-start(s32[128,1,2]{2,1,0:T(1,128)} %bitcast.11), calls=%async_computation.2 | async-start | bytes 131072 | tf_op jit(solution)/shard_map/all_to_all | solution.py:102
  190.9 45.2 %copy-start.1 = (bf16[128,768]{1,0:T(8,128)(2,1)}, bf16[128,768]{1,0:T(8,128)(2,1)S(1)}, u32[]{:S(2)}) copy-start(bf16[128,768]{1,0:T(8,128)(2,1)S(1)} %fusion.6) | copy-start | bytes 589828
  202.1 22.8 %all-to-all-start.7 = ((bf16[128,2,768]{2,1,0:T(2,128)(2,1)}), bf16[128,2,768]{2,1,0:T(2,128)(2,1)S(1)}, u32[]{:S(2)}, u32[]{:S(2)}) async-start(bf16[128,2,768]{2,1,0:T(2,128)(2,1)} %reshape.467), calls=%async_computation.7 | async-start | bytes 786432 | tf_op jit(solution)/shard_map/all_to_all | solution.py:88
  224.9 24.0 %all-to-all-start.11 = ((bf16[128,2,768]{2,1,0:T(2,128)(2,1)}), bf16[128,2,768]{2,1,0:T(2,128)(2,1)S(1)}, u32[]{:S(2)}, u32[]{:S(2)}) async-start(bf16[128,2,768]{2,1,0:T(2,128)(2,1)} %reshape.470), calls=%async_computation.11 | async-start | bytes 786432 | tf_op jit(solution)/shard_map/all_to_all | solution.py:88
  248.9 24.0 %all-to-all-start.3 = ((bf16[128,2,768]{2,1,0:T(2,128)(2,1)}), bf16[128,2,768]{2,1,0:T(2,128)(2,1)S(1)}, u32[]{:S(2)}, u32[]{:S(2)}) async-start(bf16[128,2,768]{2,1,0:T(2,128)(2,1)} %reshape.464), calls=%async_computation.3 | async-start | bytes 786432 | tf_op jit(solution)/shard_map/all_to_all | solution.py:88
  256.1 60.6 %all-reduce.3.cloned.1.call-start = ((), (), s32[]{:S(2)}) async-start(), calls=%async_computation.15 | async-start | bytes 150528 | tf_op jit(solution)/shard_map/psum | solution.py:126
  258.0 58.7 %copy-start.5 = (f32[8]{0:T(128)S(1)}, f32[8]{0:T(128)}, u32[]{:S(2)}) copy-start(f32[8]{0:T(128)} %param.25) | copy-start | bytes 100
  258.0 59.3 %copy-start.3 = (f32[8,768]{1,0:T(8,128)S(1)}, f32[8,768]{1,0:T(8,128)}, u32[]{:S(2)}) copy-start(f32[8,768]{1,0:T(8,128)} %param.24) | copy-start | bytes 73732
  426.1 7.7 %copy-start.4 = (s32[3,1,128]{2,1,0:T(1,128)S(1)}, s32[3,1,128]{2,1,0:T(1,128)}, u32[]{:S(2)}) copy-start(s32[3,1,128]{2,1,0:T(1,128)} %param.23) | copy-start | bytes 4612
  426.1 48.8 %all-to-all-start = ((bf16[128,8,768]{2,1,0:T(8,128)(2,1)}), bf16[128,8,768]{2,1,0:T(8,128)(2,1)S(1)}, u32[]{:S(2)}, u32[]{:S(2)}) async-start(bf16[128,8,768]{2,1,0:T(8,128)(2,1)} %stack.8), calls=%async_computation | async-start | bytes 3145728 | tf_op jit(solution)/shard_map/all_to_all | solution.py:121
  434.7 41.1 %copy-start.2 = (bf16[128,768]{1,0:T(8,128)(2,1)S(1)}, bf16[128,768]{1,0:T(8,128)(2,1)}, u32[]{:S(2)}) copy-start(bf16[128,768]{1,0:T(8,128)(2,1)} %copy-done.1) | copy-start | bytes 589828
Sparse Core Ops, SparseCore 0:
  10.1 43.5 all-gather.3
  55.7 30.8 all-gather.5
  88.7 31.6 all-gather.7
  274.1 42.5 all-reduce.2
